TPU v7x, 32 devices: a whole 2x2x4 slice. The times are simulated.
32 devices in a mesh: dp: 2 (over y), seq: 16 (over z, x, core).
Axes of the slice: x: 2, y: 2, z: 4, core: 2. Of those that a mesh axis runs over, the one named last changes fastest.
Arguments:
- frame_in: bfloat16 [2, 2304, 1024], P('dp', 'seq'), may hold values from -120 to 120
- token_ids: int32 [2, 16, 60], P('dp', 'seq'), may hold values from 0 to 1663
- durations: int32 [2, 16, 60], P('dp', 'seq'), may hold values from 1 to 4, 144 in all within a row
- valid_len: int32 [2], P('dp'), may hold values from 576 to 2304, as said below
- t_bin: int32 [2], P('dp'), may hold values from 0 to 63
- token_table: bfloat16 [1664, 512], P('seq'), may hold values from -6 to 6
- enc_weight: bfloat16 [512, 1024], replicated, may hold values from -0.25 to 0.25
- mod_table: float32 [64, 2048], replicated, may hold values from -1.2 to 2.5
- w_query: bfloat16 [1024, 512], P('seq'), may hold values from -0.1875 to 0.1875
- w_key: bfloat16 [1024, 512], P('seq'), may hold values from -0.1875 to 0.1875
- w_value: bfloat16 [1024, 512], P('seq'), may hold values from -0.1875 to 0.1875
- attn_grad: bfloat16 [2, 2304, 512], P('dp', 'seq'), may hold values from -6 to 6
Outputs:
- attn_out: bfloat16 [2, 2304, 512], P('dp', 'seq')
- frame_grad: bfloat16 [2, 2304, 1024], P('dp', 'seq')
- query_weight_grad: float32 [1024, 512], P('seq')
- key_weight_grad: float32 [1024, 512], P('seq')
- value_weight_grad: float32 [1024, 512], P('seq')
Inputs may be any that keep to these rules, and one draw needn't show every extreme that they name: In every slab the 60 durations sum to 144, so each token's frames lie in its own slab; some token lasts 4 frames. `valid_len`: some recording is valid over all 2304 frames.
All inputs are finite; a program needn't handle non-finite values.
Results may differ from a plain program's by a relative error of at most 0.017.
The roundings to bfloat16 on the way count: a program that leaves them out, or rounds other values in their place, can miss the bound.
Values may be sent and summed in bfloat16 or wider, within the bound.
No kernel may reach another device: no remote copies, remote signals or barrier semaphores. Data moves between devices by JAX's collectives and lax.ppermute only.
A program may use at most 64 MiB of HBM per device.

v0:
```python
import math
import jax
import jax.numpy as jnp
from jax import lax
from jax.sharding import PartitionSpec as P

D = 1024
HEADS = 8
HD = 64
BLK = 48
QW = 512


def shifted(block, axis, distance):
    devices = range(lax.axis_size(axis))
    route = [(i - distance, i) for i in devices if i - distance in devices]
    return lax.ppermute(block, axis, route)


def attend_window(
    q_blocks, key_ext, value_ext, grad_out, query_pos, key_pos, valid_end, frames_total
):
    n_blocks = q_blocks.shape[0]
    block_len = q_blocks.shape[1]
    key_win = jnp.concatenate([key_ext[offset : offset + n_blocks] for offset in range(4)], axis=1)
    value_win = jnp.concatenate(
        [value_ext[offset : offset + n_blocks] for offset in range(4)], axis=1
    )
    key_here = key_pos[:, None, :]
    allowed = (
        (key_here >= 0)
        & (key_here < frames_total)
        & ((key_here < valid_end) | (query_pos[:, :, None] >= valid_end))
    )
    row_mask = allowed[:, None]
    inv_scale = 1.0 / math.sqrt(q_blocks.shape[-1])
    scores = (
        jnp.einsum("bqhd,bkhd->bhqk", q_blocks, key_win, preferred_element_type=jnp.float32)
        * inv_scale
    )
    scores = jnp.where(row_mask, scores, -1e30)
    row_top = jnp.max(scores, axis=-1, keepdims=True)
    shifted_exp = jnp.where(row_mask, jnp.exp(scores - row_top), 0.0)
    attn_prob = shifted_exp / jnp.sum(shifted_exp, axis=-1, keepdims=True)
    probs_low = attn_prob.astype(jnp.bfloat16)
    mixed_out = jnp.einsum(
        "bhqk,bkhd->bqhd", probs_low, value_win, preferred_element_type=jnp.float32
    ).astype(jnp.bfloat16)
    grad_probs = jnp.einsum(
        "bqhd,bkhd->bhqk", grad_out, value_win, preferred_element_type=jnp.float32
    )
    centre = jnp.sum(attn_prob * grad_probs, axis=-1, keepdims=True)
    grad_scores = (attn_prob * (grad_probs - centre) * inv_scale).astype(jnp.bfloat16)
    grad_query = jnp.einsum(
        "bhqk,bkhd->bqhd", grad_scores, key_win, preferred_element_type=jnp.float32
    ).astype(jnp.bfloat16)
    key_terms = jnp.einsum(
        "bhqk,bqhd->bkhd", grad_scores, q_blocks, preferred_element_type=jnp.float32
    )
    value_terms = jnp.einsum(
        "bhqk,bqhd->bkhd", probs_low, grad_out, preferred_element_type=jnp.float32
    )
    win_terms = jnp.concatenate([key_terms, value_terms], axis=2)
    pieces = win_terms.reshape(n_blocks, 4, block_len, win_terms.shape[2], win_terms.shape[3])
    folded = jnp.zeros((n_blocks + 3,) + pieces.shape[2:], jnp.float32)
    for offset in range(4):
        folded = folded + jnp.pad(pieces[:, offset], ((offset, 3 - offset), (0, 0), (0, 0), (0, 0)))
    return (mixed_out, grad_query, folded)


def pick_rows(wanted, table_piece):
    inside = (wanted >= 0) & (wanted < table_piece.shape[0])
    picked = jnp.take(table_piece, jnp.clip(wanted, 0, table_piece.shape[0] - 1), axis=0)
    return jnp.where(inside[:, None], picked, jnp.zeros_like(picked))


def shards(
    frame_in,
    token_ids,
    durations,
    valid_len,
    t_bin,
    token_table,
    enc_weight,
    mod_table,
    w_query,
    w_key,
    w_value,
    attn_grad,
):
    frames = frame_in[0]
    n_frames = frames.shape[0]
    seq_count = lax.axis_size("seq")
    seq_index = lax.axis_index("seq")
    dp_count = lax.axis_size("dp")
    frames_total = n_frames * seq_count
    valid_end = valid_len[0]
    wanted = token_ids[0, 0]
    token_emb = pick_rows(wanted, lax.all_gather(token_table, "seq", axis=0, tiled=True))
    token_ends = jnp.cumsum(durations[0, 0])
    local_pos = jnp.arange(n_frames, dtype=jnp.int32)
    owner_tok = jnp.sum((token_ends[None, :] <= local_pos[:, None]).astype(jnp.int32), axis=1)
    frame_emb = jnp.take(token_emb, owner_tok, axis=0)
    hidden_in = frames.astype(jnp.float32) + jnp.dot(
        frame_emb, enc_weight, preferred_element_type=jnp.float32
    )
    root_ms = jnp.sqrt(jnp.mean(hidden_in * hidden_in, axis=1, keepdims=True) + 1e-06)
    normed = hidden_in / root_ms
    modulation = lax.dynamic_index_in_dim(mod_table, t_bin[0], 0, keepdims=False)
    gain_part = 1.0 + modulation[:D]
    shift_part = modulation[D:]
    modulated = (normed * gain_part + shift_part).astype(jnp.bfloat16)
    shard_cat = jnp.concatenate([w_query, w_key, w_value], axis=1)
    weights_all = lax.all_gather(shard_cat, "seq", axis=0, tiled=True)
    projected = jnp.dot(modulated, weights_all, preferred_element_type=jnp.float32).astype(
        jnp.bfloat16
    )
    queries = projected[:, :QW]
    keys_values = projected[:, QW:]
    before_rim = shifted(keys_values[n_frames - 2 * BLK :], "seq", 1)
    after_rim = shifted(keys_values[:BLK], "seq", -1)
    extended = jnp.concatenate([before_rim, keys_values, after_rim], axis=0)
    n_blocks = n_frames // BLK
    ext_blocks = extended.reshape(n_blocks + 3, BLK, 2, HEADS, HD)
    global_pos = seq_index * n_frames + local_pos
    query_pos = global_pos.reshape(n_blocks, BLK)
    key_pos = (
        seq_index * n_frames
        + (jnp.arange(n_blocks, dtype=jnp.int32)[:, None] - 2) * BLK
        + jnp.arange(4 * BLK, dtype=jnp.int32)[None, :]
    )
    live_rows = global_pos < valid_end
    grad_live = jnp.where(live_rows[:, None], attn_grad[0], jnp.zeros_like(attn_grad[0]))
    attn_blocks, query_grad, ext_grad = attend_window(
        queries.reshape(n_blocks, BLK, HEADS, HD),
        ext_blocks[:, :, 0],
        ext_blocks[:, :, 1],
        grad_live.reshape(n_blocks, BLK, HEADS, HD),
        query_pos,
        key_pos,
        valid_end,
        frames_total,
    )
    ext_rows = ext_grad.reshape(n_frames + 3 * BLK, 2 * QW)
    from_next = shifted(ext_rows[: 2 * BLK], "seq", -1)
    from_prev = shifted(ext_rows[n_frames + 2 * BLK :], "seq", 1)
    own_rows = ext_rows[2 * BLK : 2 * BLK + n_frames]
    own_rows = (
        own_rows
        + jnp.pad(from_next, ((n_frames - 2 * BLK, 0), (0, 0)))
        + jnp.pad(from_prev, ((0, n_frames - BLK), (0, 0)))
    )
    grad_cat = jnp.concatenate(
        [query_grad.reshape(n_frames, QW), own_rows.astype(jnp.bfloat16)], axis=1
    )
    grad_scale = 1.0 / math.sqrt(dp_count * frames_total)
    per_seq = lax.psum_scatter(
        (
            lax.dot_general(
                modulated, grad_cat, (((0,), (0,)), ((), ())), preferred_element_type=jnp.float32
            )
            * grad_scale
        ).astype(jnp.bfloat16),
        "seq",
        scatter_dimension=0,
        tiled=True,
    ).astype(jnp.float32)
    weight_grad = lax.psum(per_seq, "dp")
    hidden_grad = lax.dot_general(
        grad_cat, weights_all, (((1,), (1,)), ((), ())), preferred_element_type=jnp.float32
    )
    scaled_grad = hidden_grad * gain_part
    frame_grad = (
        scaled_grad - normed * jnp.mean(scaled_grad * normed, axis=1, keepdims=True)
    ) / root_ms
    return (
        attn_blocks.reshape(n_frames, QW)[None],
        frame_grad.astype(jnp.bfloat16)[None],
        weight_grad[:, :QW],
        weight_grad[:, QW : 2 * QW],
        weight_grad[:, 2 * QW :],
    )


def solution(mesh):
    placed = (
        P("dp", "seq", None),
        P("dp", "seq", None),
        P("dp", "seq", None),
        P("dp"),
        P("dp"),
        P("seq", None),
        P(),
        P(),
        P("seq", None),
        P("seq", None),
        P("seq", None),
        P("dp", "seq", None),
    )
    return jax.shard_map(
        shards,
        mesh=mesh,
        in_specs=placed,
        out_specs=(
            P("dp", "seq", None),
            P("dp", "seq", None),
            P("seq", None),
            P("seq", None),
            P("seq", None),
        ),
        check_vma=False,
    )
```

profile of v0, /device:TPU:0, one launch (start us, length us, event | category | flops | bytes accessed | tf_op | source)
XLA Modules:
  0.0 271.2 jit_solution(1181808643607981817)
XLA Ops:
  7.2 0.7 all-gather.3.cloned.1.call-update
  8.0 1.6 pad_maximum_fusion.7
  11.0 0.8 copy.50
  11.7 0.1 reduce-window.8
  11.8 0.1 reduce
  12.0 0.7 fusion.38
  12.7 0.1 convert_reduce_fusion
  12.8 0.9 dynamic-slice_add_fusion
  13.7 0.7 compare_and_fusion
  14.3 0.7 and_bitcast_fusion
  15.1 38.0 %all-gather.3.cloned.1.call-done = bf16[1664,512]{1,0:T(8,128)(2,1)} async-done(((bf16[104,512]{1,0:T(8,128)(2,1)}), bf16[1664,512]{1,0:T(8,128)(2,1)}) %all-gather.3.cloned.1.call-update) | async-done | bytes 1703952 | tf_op jit(solution)/shard_map/all_gather | solution.py:99
  53.0 2.4 gather_fusion
  55.5 0.9 gather_fusion.1
  56.4 0.5 multiply_reduce_fusion.2
  56.9 43.3 %all-gather.5.cloned.1.call-done = bf16[1024,1536]{1,0:T(8,128)(2,1)} async-done(((bf16[64,1536]{1,0:T(8,128)(2,1)}), bf16[1024,1536]{1,0:T(8,128)(2,1)}) %all-gather.5.cloned.1.call-update) | async-done | bytes 3145744 | tf_op jit(solution)/shard_map/all_gather | solution.py:114
  100.2 2.6 convolution_convert_fusion
  102.9 1.3 collective-permute-start.1
  104.2 3.0 %collective-permute-start = (bf16[96,1024]{1,0:T(8,128)(2,1)S(1)}, bf16[96,1024]{1,0:T(8,128)(2,1)S(1)}, u32[]{:S(2)}, u32[]{:S(2)}) collective-permute-start(bf16[96,1024]{1,0:T(8,128)(2,1)S(1)} %slice.158), channel_id=1, source_target_pairs={{0,1},{1,2},{2,3},{3,4},{4,5},{5,6},{6,7},{7,8},{8,9},{9,10},{10,1... | collective-permute-start | bytes 589832 | tf_op jit(solution)/shard_map/ppermute | solution.py:17
  107.3 0.9 squeeze.30
  108.3 0.9 reshape.221
  109.3 0.7 reshape.220
  110.0 1.5 fusion.53
  111.5 1.3 copy.72
  112.8 2.1 copy.74
  114.8 1.0 copy.73
  115.8 1.0 copy.71
  116.7 1.0 copy.70
  117.7 0.3 copy.69
  118.0 1.0 copy.68
  119.0 0.3 copy.75
  119.3 3.3 %fusion.55 = (f32[3,8,48]{2,1,0:T(8,128)S(1)}, f32[3,8,48,192]{3,2,1,0:T(8,128)}) fusion(pred[3,48,192]{2,1,0:T(8,128)(4,1)S(1)} %or_and_fusion, bf16[3,48,8,64]{3,2,1,0:T(8,128)(2,1)} %reshape.221, bf16[3,48,8,64]{1,3,2,0:T(8,128)(2,1)S(1)} %bitcast.84, bf16[3,48,8,64]{1,3,2,0:T(8,128)(2,1)S(1)} %bitcast.81, bf16[3,48,8,64]{1,3,2,0:T(8,128)(2,1)} %bitcast.82, ...), kind=kOutput, calls=%fused_computation.98 | convolution fusion | flops 31776960 | bytes 1654272 | tf_op jit(solution)/shard_map/sub | solution.py:43
  122.6 2.1 convolution_bitcast_fusion
  124.8 2.0 fusion.24
  126.7 10.4 %convolution_bitcast_fusion.1 = f32[3,192,8,64]{1,3,2,0:T(8,128)} fusion(f32[3,8,48,192]{3,2,1,0:T(8,128)} %fusion.24, bf16[3,48,8,64]{3,2,1,0:T(8,128)(2,1)} %reshape.221, f32[3,8,48,192]{3,2,1,0:T(8,128)} %get-tuple-element.27, f32[3,8,48]{2,1,0:T(8,128)S(1)} %get-tuple-element.26), kind=kOutput, calls=%fused_computation.10 | convolution fusion | flops 29861184 | bytes 3101184 | tf_op jit(solution)/shard_map/bhqk,bqhd->bkhd/dot_general | solution.py:57
  137.2 3.5 %pad_maximum_fusion = f32[3,192,16,64]{1,3,2,0:T(8,128)} fusion(f32[3,192,8,64]{1,3,2,0:T(8,128)S(1)} %convolution_bitcast_fusion, f32[3,192,8,64]{1,3,2,0:T(8,128)} %convolution_bitcast_fusion.1), kind=kLoop, calls=%fused_computation.5 | loop fusion | flops 589824 | bytes 4718592 | tf_op jit(solution)/shard_map/concatenate | solution.py:63
  140.6 5.9 %copy.64 = f32[3,192,16,64]{3,2,1,0:T(8,128)} copy(f32[3,192,16,64]{1,3,2,0:T(8,128)} %pad_maximum_fusion) | data formatting | bytes 4718592 | tf_op jit(solution)/shard_map/concatenate | solution.py:63
  146.5 2.7 %slice_bitcast_fusion.3 = (f32[3,48,16,64]{3,2,1,0:T(8,128)S(1)}, f32[3,48,16,64]{3,2,1,0:T(8,128)S(1)}, f32[3,48,16,64]{3,2,1,0:T(8,128)S(1)}, f32[3,48,16,64]{3,2,1,0:T(8,128)S(1)}) fusion(f32[3,4,48,16,64]{4,3,2,1,0:T(8,128)} %bitcast.69), kind=kLoop, calls=%fused_computation.26 | loop fusion | bytes 4718592 | tf_op jit(solution)/shard_map/squeeze | solution.py:67
  149.3 0.3 pad_add_fusion
  149.6 0.7 copy-done.1
  150.3 0.4 copy-done.3
  150.7 1.4 copy-done.5
  152.1 1.0 slice.175
  153.1 2.2 slice.148
  155.3 1.6 collective-permute-start.2
  156.9 0.8 pad_add_fusion.1
  157.7 1.8 slice.150
  159.5 5.2 %collective-permute-start.3 = (f32[48,1024]{1,0:T(8,128)}, f32[48,1024]{1,0:T(8,128)}, u32[]{:S(2)}, u32[]{:S(2)}) collective-permute-start(f32[48,1024]{1,0:T(8,128)} %slice.150), channel_id=1, source_target_pairs={{0,1},{1,2},{2,3},{3,4},{4,5},{5,6},{6,7},{7,8},{8,9},{9,10},{10,1... | collective-permute-start | bytes 589832 | tf_op jit(solution)/shard_map/ppermute | solution.py:17
  164.8 10.3 %fusion.11 = bf16[3,48,8,64]{3,1,2,0:T(8,128)(2,1)S(1)} fusion(f32[3,8,48,192]{3,2,1,0:T(8,128)} %fusion.24, bf16[3,48,8,64]{1,3,2,0:T(8,128)(2,1)} %bitcast.85, bf16[3,48,8,64]{1,3,2,0:T(8,128)(2,1)} %bitcast.80, bf16[3,48,8,64]{1,3,2,0:T(8,128)(2,1)} %bitcast.83, bf16[3,48,8,64]{1,3,2,0:T(8,128)(2,1)} %bitcast.79, ...), kind=kOutput, calls=%fused_computation.28 | convolution fusion | flops 32294208 | bytes 2511360 | tf_op jit(solution)/shard_map/bhqk,bkhd->bqhd/dot_general | solution.py:54
  175.1 0.2 reshape.222
  175.4 0.3 slice.146
  175.8 1.2 add_convert_fusion
  176.9 0.7 copy-done.23
  177.7 2.7 %multiply_convert_fusion = bf16[1024,1536]{1,0:T(8,128)(2,1)} fusion(bf16[144,1024]{1,0:T(8,128)(2,1)S(1)} %add_convert_fusion, bf16[144,512]{1,0:T(8,128)(2,1)S(1)} %reshape.222, f32[1024]{0:T(1024)S(1)} %bitcast.90, f32[1024]{0:T(1024)S(1)} %bitcast.87, f32[144,1024]{1,0:T(8,128)S(1)} %copy-done.7, f32[144]{0:T(256)S(1)} %copy-done.31), kind=kOutput, calls=%fused_computation.4 | convolution fusion | flops 457605120 | bytes 4186688 | tf_op jit(solution)/shard_map/dot_general | solution.py:159
  180.5 0.9 copy-done.11
  181.4 0.1 copy-done.13
  181.5 0.1 copy-done.15
  181.6 0.1 copy-done.17
  181.8 2.2 fusion.10
  184.0 0.9 broadcast_in_dim_reshape.4
  184.9 3.3 %multiply_reduce_fusion.1 = (f32[144]{0:T(256)S(1)}, f32[144,1024]{1,0:T(8,128)S(1)}) fusion(f32[144,1024]{1,0:T(8,128)S(1)} %copy-done.7, f32[144]{0:T(256)S(1)} %copy-done.32, f32[1024]{0:T(1024)S(1)} %bitcast.88, bf16[1024,1536]{1,0:T(8,128)(2,1)} %all-gather.5.cloned.1.call-done, bf16[144,1024]{1,0:T(8,128)(2,1)} %copy-done.23, ...), kind=kOutput, calls=%fused_computation.35 | convolution fusion | flops 454459264 | bytes 4772992 | tf_op jit(solution)/shard_map/dot_general | solution.py:169
  188.2 0.9 fusion.21
  189.1 59.4 %reduce-scatter.2.cloned.1.call-done = bf16[64,1536]{1,0:T(8,128)(2,1)} async-done(((bf16[1024,1536]{1,0:T(8,128)(2,1)}), bf16[64,1536]{1,0:T(8,128)(2,1)}) %reduce-scatter.2.cloned.1.call-update) | async-done | bytes 196624 | tf_op jit(solution)/shard_map/reduce_scatter | solution.py:157
  248.5 15.4 %all-reduce.7 = f32[64,1536]{1,0:T(8,128)S(1)} all-reduce(bf16[64,1536]{1,0:T(8,128)(2,1)} %reduce-scatter.2.cloned.1.call-done), channel_id=1, replica_groups=mesh['dp'=2,'seq'=16] {'dp'}, use_global_device_ids=true, to_apply=%region_8.9 | all-reduce | flops 98304 | bytes 589824 | tf_op jit(solution)/shard_map/psum | solution.py:168
  263.9 0.8 fusion.54
  (93 shorter events, 0.9 us)
Async XLA Ops:
  7.2 49.2 %copy-start = (bf16[512,1024]{1,0:T(8,128)(2,1)S(1)}, bf16[512,1024]{1,0:T(8,128)(2,1)}, u32[]{:S(2)}) copy-start(bf16[512,1024]{1,0:T(8,128)(2,1)} %param.18) | copy-start | bytes 3145732
  7.2 45.9 %all-gather.3.cloned.1.call-start = ((), (), s32[]{:S(2)}) async-start(), calls=%async_computation.1 | async-start | bytes 1810432 | tf_op jit(solution)/shard_map/all_gather | solution.py:99
  7.9 92.3 %all-gather.5.cloned.1.call-start = ((), (), s32[]{:S(2)}) async-start(), calls=%async_computation.2 | async-start | bytes 3342336 | tf_op jit(solution)/shard_map/all_gather | solution.py:114
  9.6 46.8 %copy-start.22 = (bf16[1,144,1024]{2,1,0:T(8,128)(2,1)S(1)}, bf16[1,144,1024]{2,1,0:T(8,128)(2,1)}, u32[]{:S(2)}) copy-start(bf16[1,144,1024]{2,1,0:T(8,128)(2,1)} %param.12) | copy-start | bytes 884740
  9.6 238.9 %reduce-scatter.2.cloned.1.call-start = ((), (), s32[]{:S(2)}) async-start(), calls=%async_computation.3 | async-start | bytes 3342336 | tf_op jit(solution)/shard_map/reduce_scatter | solution.py:157
  13.6 86.6 %copy-start.25 = (f32[1,1024]{1,0:T(1,128)}, f32[1,1024]{1,0:T(1,128)S(1)}, u32[]{:S(2)}) copy-start(f32[1,1024]{1,0:T(1,128)S(1)} %get-tuple-element.17) | copy-start | bytes 12292
  13.6 86.6 %copy-start.28 = (f32[1,1024]{1,0:T(1,128)}, f32[1,1024]{1,0:T(1,128)S(1)}, u32[]{:S(2)}) copy-start(f32[1,1024]{1,0:T(1,128)S(1)} %get-tuple-element.18) | copy-start | bytes 12292
  56.9 45.9 %copy-start.6 = (f32[144,1024]{1,0:T(8,128)}, f32[144,1024]{1,0:T(8,128)S(1)}, u32[]{:S(2)}) copy-start(f32[144,1024]{1,0:T(8,128)S(1)} %get-tuple-element.25) | copy-start | bytes 1769476
  56.9 43.3 %copy-start.30 = (f32[144]{0:T(256)}, f32[144]{0:T(256)S(1)}, u32[]{:S(2)}) copy-start(f32[144]{0:T(256)S(1)} %add_sqrt_fusion) | copy-start | bytes 1732
  100.2 7.1 %copy-start.24 = (bf16[1,144,512]{2,1,0:T(8,128)(2,1)S(1)}, bf16[1,144,512]{2,1,0:T(8,128)(2,1)}, u32[]{:S(2)}) copy-start(bf16[1,144,512]{2,1,0:T(8,128)(2,1)} %param.23) | copy-start | bytes 442372
  102.9 6.3 %collective-permute-start.1 = (bf16[48,1024]{1,0:T(8,128)(2,1)S(1)}, bf16[48,1024]{1,0:T(8,128)(2,1)S(1)}, u32[]{:S(2)}, u32[]{:S(2)}) collective-permute-start(bf16[48,1024]{1,0:T(8,128)(2,1)S(1)} %slice.160), channel_id=1, source_target_pairs={{1,0},{2,1},{3,2},{4,3},{5,4},{6,5},{7,6},{8,7},{9,8},{10,9},{11,1... | collective-permute-start | bytes 294920 | tf_op jit(solution)/shard_map/ppermute | solution.py:17
  104.2 5.0 %collective-permute-start = (bf16[96,1024]{1,0:T(8,128)(2,1)S(1)}, bf16[96,1024]{1,0:T(8,128)(2,1)S(1)}, u32[]{:S(2)}, u32[]{:S(2)}) collective-permute-start(bf16[96,1024]{1,0:T(8,128)(2,1)S(1)} %slice.158), channel_id=1, source_target_pairs={{0,1},{1,2},{2,3},{3,4},{4,5},{5,6},{6,7},{7,8},{8,9},{9,10},{10,1... | collective-permute-start | bytes 589832 | tf_op jit(solution)/shard_map/ppermute | solution.py:17
  111.5 3.3 %copy-start.9 = (bf16[3,48,1,8,64]{4,3,2,1,0:T(8,128)(2,1)S(1)}, bf16[3,48,1,8,64]{4,3,2,1,0:T(8,128)(2,1)}, u32[]{:S(2)}) copy-start(bf16[3,48,1,8,64]{4,3,2,1,0:T(8,128)(2,1)} %get-tuple-element.11) | copy-start | bytes 442372
  111.5 4.3 %copy-start.8 = (bf16[3,48,1,8,64]{4,3,2,1,0:T(8,128)(2,1)S(1)}, bf16[3,48,1,8,64]{4,3,2,1,0:T(8,128)(2,1)}, u32[]{:S(2)}) copy-start(bf16[3,48,1,8,64]{4,3,2,1,0:T(8,128)(2,1)} %get-tuple-element.12) | copy-start | bytes 442372
  112.7 6.6 %copy-start.18 = (bf16[3,48,1,8,64]{1,4,3,0,2:T(8,128)(2,1)}, bf16[3,48,1,8,64]{1,4,3,0,2:T(8,128)(2,1)S(1)}, u32[]{:S(2)}) copy-start(bf16[3,48,1,8,64]{1,4,3,0,2:T(8,128)(2,1)S(1)} %copy.72) | copy-start | bytes 442372
  117.7 1.6 copy-start.19
  118.0 6.7 %copy-start.14 = (bf16[3,48,1,8,64]{1,4,3,0,2:T(8,128)(2,1)}, bf16[3,48,1,8,64]{1,4,3,0,2:T(8,128)(2,1)S(1)}, u32[]{:S(2)}) copy-start(bf16[3,48,1,8,64]{1,4,3,0,2:T(8,128)(2,1)S(1)} %copy.69) | copy-start | bytes 442372
  119.3 3.3 %copy-start.20 = (bf16[3,48,1,8,64]{1,4,3,0,2:T(8,128)(2,1)}, bf16[3,48,1,8,64]{1,4,3,0,2:T(8,128)(2,1)S(1)}, u32[]{:S(2)}) copy-start(bf16[3,48,1,8,64]{1,4,3,0,2:T(8,128)(2,1)S(1)} %copy.75) | copy-start | bytes 442372
  122.6 4.1 %copy-start.33 = (f32[3,8,48]{2,1,0:T(8,128)}, f32[3,8,48]{2,1,0:T(8,128)S(1)}, u32[]{:S(2)}) copy-start(f32[3,8,48]{2,1,0:T(8,128)S(1)} %get-tuple-element.26) | copy-start | bytes 13828
  122.6 2.1 copy-start.10
  122.6 2.1 copy-start.12
  122.6 2.1 copy-start.16
  122.6 2.1 copy-start.21
  149.2 1.0 copy-start.1
  149.3 1.4 copy-start.3
  150.7 1.4 copy-start.5
  155.3 1.6 copy-start.2
  155.3 1.6 copy-start.4
  155.3 20.5 %collective-permute-start.2 = (f32[96,1024]{1,0:T(8,128)}, f32[96,1024]{1,0:T(8,128)}, u32[]{:S(2)}, u32[]{:S(2)}) collective-permute-start(f32[96,1024]{1,0:T(8,128)} %slice.148), channel_id=1, source_target_pairs={{1,0},{2,1},{3,2},{4,3},{5,4},{6,5},{7,6},{8,7},{9,8},{10,9},{11,1... | collective-permute-start | bytes 1179656 | tf_op jit(solution)/shard_map/ppermute | solution.py:17
  156.9 7.9 %copy-start.34 = (f32[3,8,48]{2,1,0:T(8,128)S(1)}, f32[3,8,48]{2,1,0:T(8,128)}, u32[]{:S(2)}) copy-start(f32[3,8,48]{2,1,0:T(8,128)} %copy-done.33) | copy-start | bytes 13828
  159.5 16.2 %collective-permute-start.3 = (f32[48,1024]{1,0:T(8,128)}, f32[48,1024]{1,0:T(8,128)}, u32[]{:S(2)}, u32[]{:S(2)}) collective-permute-start(f32[48,1024]{1,0:T(8,128)} %slice.150), channel_id=1, source_target_pairs={{0,1},{1,2},{2,3},{3,4},{4,5},{5,6},{6,7},{7,8},{8,9},{9,10},{10,1... | collective-permute-start | bytes 589832 | tf_op jit(solution)/shard_map/ppermute | solution.py:17
  164.8 10.6 %slice-start = ((f32[6,48,16,64]{3,2,1,0:T(8,128)}), f32[3,48,16,64]{3,2,1,0:T(8,128)S(1)}, s32[]{:S(2)}) async-start(f32[6,48,16,64]{3,2,1,0:T(8,128)} %copy-done.5), calls=%async_computation.4 | async-start | bytes 2359296 | tf_op jit(solution)/shard_map/slice | solution.py:147
  175.4 2.3 copy-start.7
  175.7 1.9 copy-start.26
  175.7 1.9 copy-start.29
  175.7 1.9 copy-start.31
  176.9 0.7 copy-start.23
  180.4 1.0 copy-start.11
  180.4 1.1 copy-start.13
  180.4 1.2 copy-start.15
  180.4 1.3 copy-start.17
  180.4 1.3 copy-start.35
  181.8 3.2 %copy-start.27 = (f32[1,1024]{1,0:T(1,128)S(1)}, f32[1,1024]{1,0:T(1,128)}, u32[]{:S(2)}) copy-start(f32[1,1024]{1,0:T(1,128)} %copy-done.25) | copy-start | bytes 12292
  181.8 3.2 %copy-start.32 = (f32[144]{0:T(256)S(1)}, f32[144]{0:T(256)}, u32[]{:S(2)}) copy-start(f32[144]{0:T(256)} %copy-done.30) | copy-start | bytes 1732
Sparse Core Ops, SparseCore 0:
  10.3 42.7 all-gather.2
  55.9 44.2 all-gather.4
  180.6 67.9 reduce-scatter.1
where the time goes:
time: 272 us; the launch traced here: 271 us
  waiting for transfers between devices  141 us (52%)
  matrix products  39.3 us (14%)
  local copies, waits for them, and re-layouts  36.5 us (13%)
  between operations  15.6 us (6%)
  blocking collectives  15.4 us (6%)
  other arithmetic  11.7 us (4%)
  starting transfers between devices  11.3 us (4%)
    reduce_scatter x1, waiting for transfers between devices, shards(): lax.psum_scatter((lax.dot_general(modulated, grad_cat, (((0,), (0,)), (()...  59.4 us
    all_gather x1, waiting for transfers between devices, shards(): weights_all = lax.all_gather(shard_cat, 'seq', axis=0, tiled=True)  43.3 us
    all_gather x1, waiting for transfers between devices, shards(): lax.all_gather(token_table, 'seq', axis=0, tiled=True)  38 us
    psum x1, blocking collectives, shards(): weight_grad = lax.psum(per_seq, 'dp')  15.4 us
    unnamed x80, local copies, waits for them, and re-layouts  12.5 us
    ppermute x4, starting transfers between devices, shifted(): return lax.ppermute(block, axis, route)  11.2 us
    dot_general x1, matrix products, attend_window(): jnp.einsum('bhqk,bqhd->bkhd', grad_scores, q_blocks, preferred_element_ty...  10.4 us
    dot_general x1, matrix products, attend_window(): jnp.einsum('bhqk,bkhd->bqhd', grad_scores, key_win, preferred_element_typ...  10.3 us
  transfers between devices with their start and end apart: 7, of which 3 were waited for; matrix products, arithmetic and copies ran while one was open for 12% of the time, Pallas kernels for 0%

commit v1 on v0

--- a/solution.py
+++ b/solution.py
@@ -165,7 +165,7 @@
         scatter_dimension=0,
         tiled=True,
     ).astype(jnp.float32)
-    weight_grad = lax.psum(per_seq, "dp")
+    weight_grad = per_seq + lax.ppermute(per_seq, "dp", [(0, 1), (1, 0)])
     hidden_grad = lax.dot_general(
         grad_cat, weights_all, (((1,), (1,)), ((), ())), preferred_element_type=jnp.float32
     )

time: 272 us -> 267 us (0.982)
  blocking collectives: 15.4 us -> 0 us
  waiting for transfers between devices: 141 us -> 149 us
    psum x1 -> x0, blocking collectives: 15.4 us -> none  [shards(): weight_grad = lax.psum(per_seq, 'dp')]
    ppermute x0 -> x1, waiting for transfers between devices: none -> 6.58 us  [shards(): weight_grad = per_seq + lax.ppermute(per_seq, 'dp', [(0, 1), (1, 0)])]
    unnamed x80 -> x82, local copies, waits for them, and re-layouts: 12.5 us -> 12.5 us
  transfers between devices with their start and end apart: 7 -> 8, of which waited for: 3 -> 4; matrix products, arithmetic and copies ran while one was open for 12% -> 12% of each run, Pallas kernels for 0% -> 0%
where the time goes in v1:
time: 267 us; the launch traced here: 266 us
  waiting for transfers between devices  149 us (56%)
  matrix products  39.3 us (15%)
  local copies, waits for them, and re-layouts  36.5 us (14%)
  between operations  15.6 us (6%)
  starting transfers between devices  12.9 us (5%)
  other arithmetic  12.8 us (5%)
    reduce_scatter x1, waiting for transfers between devices, shards(): lax.psum_scatter((lax.dot_general(modulated, grad_cat, (((0,), (0,)), (()...  60.3 us
    all_gather x1, waiting for transfers between devices, shards(): weights_all = lax.all_gather(shard_cat, 'seq', axis=0, tiled=True)  43.3 us
    all_gather x1, waiting for transfers between devices, shards(): lax.all_gather(token_table, 'seq', axis=0, tiled=True)  38 us
    unnamed x82, local copies, waits for them, and re-layouts  12.5 us
    ppermute x4, starting transfers between devices, shifted(): return lax.ppermute(block, axis, route)  11.2 us
    dot_general x1, matrix products, attend_window(): jnp.einsum('bhqk,bqhd->bkhd', grad_scores, q_blocks, preferred_element_ty...  10.4 us
    dot_general x1, matrix products, attend_window(): jnp.einsum('bhqk,bkhd->bqhd', grad_scores, key_win, preferred_element_typ...  10.3 us
    ppermute x1, waiting for transfers between devices, shards(): weight_grad = per_seq + lax.ppermute(per_seq, 'dp', [(0, 1), (1, 0)])  6.58 us
  transfers between devices with their start and end apart: 8, of which 4 were waited for; matrix products, arithmetic and copies ran while one was open for 12% of the time, Pallas kernels for 0%

profile of v1, /device:TPU:0, one launch (start us, length us, event | category | flops | bytes accessed | tf_op | source)
XLA Modules:
  0.0 265.9 jit_solution(11017096866380035656)
XLA Ops:
  7.2 0.7 all-gather.3.cloned.1.call-update
  8.0 1.6 pad_maximum_fusion.7
  11.0 0.8 copy.50
  11.8 0.1 reduce
  12.0 0.7 fusion.38
  12.8 0.9 dynamic-slice_add_fusion
  13.7 0.7 compare_and_fusion
  14.3 0.7 and_bitcast_fusion
  15.1 38.0 %all-gather.3.cloned.1.call-done = bf16[1664,512]{1,0:T(8,128)(2,1)} async-done(((bf16[104,512]{1,0:T(8,128)(2,1)}), bf16[1664,512]{1,0:T(8,128)(2,1)}) %all-gather.3.cloned.1.call-update) | async-done | bytes 1703952 | tf_op jit(solution)/shard_map/all_gather | solution.py:99
  53.0 2.4 gather_fusion
  55.5 0.9 gather_fusion.1
  56.4 0.5 multiply_reduce_fusion.2
  56.9 43.3 %all-gather.5.cloned.1.call-done = bf16[1024,1536]{1,0:T(8,128)(2,1)} async-done(((bf16[64,1536]{1,0:T(8,128)(2,1)}), bf16[1024,1536]{1,0:T(8,128)(2,1)}) %all-gather.5.cloned.1.call-update) | async-done | bytes 3145744 | tf_op jit(solution)/shard_map/all_gather | solution.py:114
  100.2 2.6 convolution_convert_fusion
  102.9 1.3 collective-permute-start.1
  104.2 3.0 %collective-permute-start = (bf16[96,1024]{1,0:T(8,128)(2,1)S(1)}, bf16[96,1024]{1,0:T(8,128)(2,1)S(1)}, u32[]{:S(2)}, u32[]{:S(2)}) collective-permute-start(bf16[96,1024]{1,0:T(8,128)(2,1)S(1)} %slice.158), channel_id=1, source_target_pairs={{0,1},{1,2},{2,3},{3,4},{4,5},{5,6},{6,7},{7,8},{8,9},{9,10},{10,1... | collective-permute-start | bytes 589832 | tf_op jit(solution)/shard_map/ppermute | solution.py:17
  107.3 0.9 squeeze.30
  108.3 0.9 reshape.221
  109.3 0.7 reshape.220
  110.0 1.4 fusion.53
  111.4 1.3 copy.72
  112.7 2.1 copy.74
  114.8 1.0 copy.73
  115.8 1.0 copy.71
  116.8 1.0 copy.70
  117.8 0.3 copy.69
  118.0 1.0 copy.68
  119.0 0.3 copy.75
  119.3 3.3 %fusion.55 = (f32[3,8,48]{2,1,0:T(8,128)S(1)}, f32[3,8,48,192]{3,2,1,0:T(8,128)}) fusion(pred[3,48,192]{2,1,0:T(8,128)(4,1)S(1)} %or_and_fusion, bf16[3,48,8,64]{3,2,1,0:T(8,128)(2,1)} %reshape.221, bf16[3,48,8,64]{1,3,2,0:T(8,128)(2,1)S(1)} %bitcast.84, bf16[3,48,8,64]{1,3,2,0:T(8,128)(2,1)S(1)} %bitcast.81, bf16[3,48,8,64]{1,3,2,0:T(8,128)(2,1)} %bitcast.82, ...), kind=kOutput, calls=%fused_computation.99 | convolution fusion | flops 31776960 | bytes 1654272 | tf_op jit(solution)/shard_map/sub | solution.py:43
  122.6 2.1 convolution_bitcast_fusion
  124.8 1.9 fusion.24
  126.7 10.4 %convolution_bitcast_fusion.1 = f32[3,192,8,64]{1,3,2,0:T(8,128)} fusion(f32[3,8,48,192]{3,2,1,0:T(8,128)} %fusion.24, bf16[3,48,8,64]{3,2,1,0:T(8,128)(2,1)} %reshape.221, f32[3,8,48,192]{3,2,1,0:T(8,128)} %get-tuple-element.27, f32[3,8,48]{2,1,0:T(8,128)S(1)} %get-tuple-element.26), kind=kOutput, calls=%fused_computation.10 | convolution fusion | flops 29861184 | bytes 3101184 | tf_op jit(solution)/shard_map/bhqk,bqhd->bkhd/dot_general | solution.py:57
  137.1 3.5 %pad_maximum_fusion = f32[3,192,16,64]{1,3,2,0:T(8,128)} fusion(f32[3,192,8,64]{1,3,2,0:T(8,128)S(1)} %convolution_bitcast_fusion, f32[3,192,8,64]{1,3,2,0:T(8,128)} %convolution_bitcast_fusion.1), kind=kLoop, calls=%fused_computation.5 | loop fusion | flops 589824 | bytes 4718592 | tf_op jit(solution)/shard_map/concatenate | solution.py:63
  140.6 5.9 %copy.64 = f32[3,192,16,64]{3,2,1,0:T(8,128)} copy(f32[3,192,16,64]{1,3,2,0:T(8,128)} %pad_maximum_fusion) | data formatting | bytes 4718592 | tf_op jit(solution)/shard_map/concatenate | solution.py:63
  146.5 2.7 %slice_bitcast_fusion.3 = (f32[3,48,16,64]{3,2,1,0:T(8,128)S(1)}, f32[3,48,16,64]{3,2,1,0:T(8,128)S(1)}, f32[3,48,16,64]{3,2,1,0:T(8,128)S(1)}, f32[3,48,16,64]{3,2,1,0:T(8,128)S(1)}) fusion(f32[3,4,48,16,64]{4,3,2,1,0:T(8,128)} %bitcast.69), kind=kLoop, calls=%fused_computation.26 | loop fusion | bytes 4718592 | tf_op jit(solution)/shard_map/squeeze | solution.py:67
  149.2 0.3 pad_add_fusion
  149.6 0.7 copy-done.1
  150.3 0.4 copy-done.3
  150.7 1.4 copy-done.5
  152.1 1.0 slice.175
  153.1 2.2 slice.148
  155.2 1.6 collective-permute-start.2
  156.9 0.8 pad_add_fusion.1
  157.7 1.8 slice.150
  159.5 5.3 %collective-permute-start.3 = (f32[48,1024]{1,0:T(8,128)}, f32[48,1024]{1,0:T(8,128)}, u32[]{:S(2)}, u32[]{:S(2)}) collective-permute-start(f32[48,1024]{1,0:T(8,128)} %slice.150), channel_id=1, source_target_pairs={{0,1},{1,2},{2,3},{3,4},{4,5},{5,6},{6,7},{7,8},{8,9},{9,10},{10,1... | collective-permute-start | bytes 589832 | tf_op jit(solution)/shard_map/ppermute | solution.py:17
  164.7 10.3 %fusion.11 = bf16[3,48,8,64]{3,1,2,0:T(8,128)(2,1)S(1)} fusion(f32[3,8,48,192]{3,2,1,0:T(8,128)} %fusion.24, bf16[3,48,8,64]{1,3,2,0:T(8,128)(2,1)} %bitcast.85, bf16[3,48,8,64]{1,3,2,0:T(8,128)(2,1)} %bitcast.80, bf16[3,48,8,64]{1,3,2,0:T(8,128)(2,1)} %bitcast.83, bf16[3,48,8,64]{1,3,2,0:T(8,128)(2,1)} %bitcast.79, ...), kind=kOutput, calls=%fused_computation.28 | convolution fusion | flops 32294208 | bytes 2511360 | tf_op jit(solution)/shard_map/bhqk,bkhd->bqhd/dot_general | solution.py:54
  175.1 0.2 reshape.222
  175.4 0.3 slice.146
  175.8 1.2 add_convert_fusion
  176.9 0.7 copy-done.24
  177.7 2.7 %multiply_convert_fusion = bf16[1024,1536]{1,0:T(8,128)(2,1)} fusion(bf16[144,1024]{1,0:T(8,128)(2,1)S(1)} %add_convert_fusion, bf16[144,512]{1,0:T(8,128)(2,1)S(1)} %reshape.222, f32[1024]{0:T(1024)S(1)} %bitcast.90, f32[1024]{0:T(1024)S(1)} %bitcast.87, f32[144,1024]{1,0:T(8,128)S(1)} %copy-done.7, f32[144]{0:T(256)S(1)} %copy-done.32), kind=kOutput, calls=%fused_computation.4 | convolution fusion | flops 457605120 | bytes 4186688 | tf_op jit(solution)/shard_map/dot_general | solution.py:159
  180.4 0.9 copy-done.12
  181.4 0.1 copy-done.14
  181.5 0.1 copy-done.16
  181.6 0.1 copy-done.18
  181.8 2.2 fusion.10
  184.0 0.9 broadcast_in_dim_reshape.4
  184.9 3.3 %multiply_reduce_fusion.1 = (f32[144]{0:T(256)S(1)}, f32[144,1024]{1,0:T(8,128)S(1)}) fusion(f32[144,1024]{1,0:T(8,128)S(1)} %copy-done.7, f32[144]{0:T(256)S(1)} %copy-done.33, f32[1024]{0:T(1024)S(1)} %bitcast.88, bf16[1024,1536]{1,0:T(8,128)(2,1)} %all-gather.5.cloned.1.call-done, bf16[144,1024]{1,0:T(8,128)(2,1)} %copy-done.24, ...), kind=kOutput, calls=%fused_computation.35 | convolution fusion | flops 454459264 | bytes 4772992 | tf_op jit(solution)/shard_map/dot_general | solution.py:169
  188.2 60.3 %reduce-scatter.2.cloned.1.call-done = bf16[64,1536]{1,0:T(8,128)(2,1)} async-done(((bf16[1024,1536]{1,0:T(8,128)(2,1)}), bf16[64,1536]{1,0:T(8,128)(2,1)}) %reduce-scatter.2.cloned.1.call-update) | async-done | bytes 196624 | tf_op jit(solution)/shard_map/reduce_scatter | solution.py:157
  248.5 1.0 convert_element_type.71
  249.6 1.5 collective-permute-start.4
  251.1 0.9 fusion.21
  252.0 6.6 %collective-permute-done.4 = f32[64,1536]{1,0:T(8,128)S(1)} collective-permute-done((f32[64,1536]{1,0:T(8,128)S(1)}, f32[64,1536]{1,0:T(8,128)S(1)}, u32[]{:S(2)}, u32[]{:S(2)}) %collective-permute-start.4) | collective-permute-done | bytes 393248 | tf_op jit(solution)/shard_map/ppermute | solution.py:168
  258.6 0.8 fusion.54
  (98 shorter events, 1.1 us)
Async XLA Ops:
  7.2 49.2 %copy-start = (bf16[512,1024]{1,0:T(8,128)(2,1)S(1)}, bf16[512,1024]{1,0:T(8,128)(2,1)}, u32[]{:S(2)}) copy-start(bf16[512,1024]{1,0:T(8,128)(2,1)} %param.18) | copy-start | bytes 3145732
  7.2 45.9 %all-gather.3.cloned.1.call-start = ((), (), s32[]{:S(2)}) async-start(), calls=%async_computation.1 | async-start | bytes 1810432 | tf_op jit(solution)/shard_map/all_gather | solution.py:99
  7.9 92.3 %all-gather.5.cloned.1.call-start = ((), (), s32[]{:S(2)}) async-start(), calls=%async_computation.2 | async-start | bytes 3342336 | tf_op jit(solution)/shard_map/all_gather | solution.py:114
  9.6 46.8 %copy-start.23 = (bf16[1,144,1024]{2,1,0:T(8,128)(2,1)S(1)}, bf16[1,144,1024]{2,1,0:T(8,128)(2,1)}, u32[]{:S(2)}) copy-start(bf16[1,144,1024]{2,1,0:T(8,128)(2,1)} %param.12) | copy-start | bytes 884740
  9.6 238.9 %reduce-scatter.2.cloned.1.call-start = ((), (), s32[]{:S(2)}) async-start(), calls=%async_computation.3 | async-start | bytes 3342336 | tf_op jit(solution)/shard_map/reduce_scatter | solution.py:157
  13.6 86.6 %copy-start.26 = (f32[1,1024]{1,0:T(1,128)}, f32[1,1024]{1,0:T(1,128)S(1)}, u32[]{:S(2)}) copy-start(f32[1,1024]{1,0:T(1,128)S(1)} %get-tuple-element.17) | copy-start | bytes 12292
  13.6 86.6 %copy-start.29 = (f32[1,1024]{1,0:T(1,128)}, f32[1,1024]{1,0:T(1,128)S(1)}, u32[]{:S(2)}) copy-start(f32[1,1024]{1,0:T(1,128)S(1)} %get-tuple-element.18) | copy-start | bytes 12292
  56.9 45.9 %copy-start.6 = (f32[144,1024]{1,0:T(8,128)}, f32[144,1024]{1,0:T(8,128)S(1)}, u32[]{:S(2)}) copy-start(f32[144,1024]{1,0:T(8,128)S(1)} %get-tuple-element.25) | copy-start | bytes 1769476
  56.9 43.3 %copy-start.31 = (f32[144]{0:T(256)}, f32[144]{0:T(256)S(1)}, u32[]{:S(2)}) copy-start(f32[144]{0:T(256)S(1)} %add_sqrt_fusion) | copy-start | bytes 1732
  100.2 7.1 %copy-start.25 = (bf16[1,144,512]{2,1,0:T(8,128)(2,1)S(1)}, bf16[1,144,512]{2,1,0:T(8,128)(2,1)}, u32[]{:S(2)}) copy-start(bf16[1,144,512]{2,1,0:T(8,128)(2,1)} %param.23) | copy-start | bytes 442372
  102.9 6.3 %collective-permute-start.1 = (bf16[48,1024]{1,0:T(8,128)(2,1)S(1)}, bf16[48,1024]{1,0:T(8,128)(2,1)S(1)}, u32[]{:S(2)}, u32[]{:S(2)}) collective-permute-start(bf16[48,1024]{1,0:T(8,128)(2,1)S(1)} %slice.160), channel_id=1, source_target_pairs={{1,0},{2,1},{3,2},{4,3},{5,4},{6,5},{7,6},{8,7},{9,8},{10,9},{11,1... | collective-permute-start | bytes 294920 | tf_op jit(solution)/shard_map/ppermute | solution.py:17
  104.2 5.0 %collective-permute-start = (bf16[96,1024]{1,0:T(8,128)(2,1)S(1)}, bf16[96,1024]{1,0:T(8,128)(2,1)S(1)}, u32[]{:S(2)}, u32[]{:S(2)}) collective-permute-start(bf16[96,1024]{1,0:T(8,128)(2,1)S(1)} %slice.158), channel_id=1, source_target_pairs={{0,1},{1,2},{2,3},{3,4},{4,5},{5,6},{6,7},{7,8},{8,9},{9,10},{10,1... | collective-permute-start | bytes 589832 | tf_op jit(solution)/shard_map/ppermute | solution.py:17
  111.4 3.4 %copy-start.9 = (bf16[3,48,1,8,64]{4,3,2,1,0:T(8,128)(2,1)S(1)}, bf16[3,48,1,8,64]{4,3,2,1,0:T(8,128)(2,1)}, u32[]{:S(2)}) copy-start(bf16[3,48,1,8,64]{4,3,2,1,0:T(8,128)(2,1)} %get-tuple-element.11) | copy-start | bytes 442372
  111.4 4.4 %copy-start.8 = (bf16[3,48,1,8,64]{4,3,2,1,0:T(8,128)(2,1)S(1)}, bf16[3,48,1,8,64]{4,3,2,1,0:T(8,128)(2,1)}, u32[]{:S(2)}) copy-start(bf16[3,48,1,8,64]{4,3,2,1,0:T(8,128)(2,1)} %get-tuple-element.12) | copy-start | bytes 442372
  112.7 6.6 %copy-start.19 = (bf16[3,48,1,8,64]{1,4,3,0,2:T(8,128)(2,1)}, bf16[3,48,1,8,64]{1,4,3,0,2:T(8,128)(2,1)S(1)}, u32[]{:S(2)}) copy-start(bf16[3,48,1,8,64]{1,4,3,0,2:T(8,128)(2,1)S(1)} %copy.72) | copy-start | bytes 442372
  117.8 1.6 copy-start.20
  118.0 6.7 %copy-start.15 = (bf16[3,48,1,8,64]{1,4,3,0,2:T(8,128)(2,1)}, bf16[3,48,1,8,64]{1,4,3,0,2:T(8,128)(2,1)S(1)}, u32[]{:S(2)}) copy-start(bf16[3,48,1,8,64]{1,4,3,0,2:T(8,128)(2,1)S(1)} %copy.69) | copy-start | bytes 442372
  119.3 3.3 %copy-start.21 = (bf16[3,48,1,8,64]{1,4,3,0,2:T(8,128)(2,1)}, bf16[3,48,1,8,64]{1,4,3,0,2:T(8,128)(2,1)S(1)}, u32[]{:S(2)}) copy-start(bf16[3,48,1,8,64]{1,4,3,0,2:T(8,128)(2,1)S(1)} %copy.75) | copy-start | bytes 442372
  122.6 4.1 %copy-start.34 = (f32[3,8,48]{2,1,0:T(8,128)}, f32[3,8,48]{2,1,0:T(8,128)S(1)}, u32[]{:S(2)}) copy-start(f32[3,8,48]{2,1,0:T(8,128)S(1)} %get-tuple-element.26) | copy-start | bytes 13828
  122.6 2.1 copy-start.11
  122.6 2.1 copy-start.13
  122.6 2.1 copy-start.17
  122.6 2.1 copy-start.22
  149.2 1.0 copy-start.1
  149.2 1.4 copy-start.3
  150.7 1.4 copy-start.5
  155.2 1.6 copy-start.2
  155.2 1.6 copy-start.4
  155.2 20.5 %collective-permute-start.2 = (f32[96,1024]{1,0:T(8,128)}, f32[96,1024]{1,0:T(8,128)}, u32[]{:S(2)}, u32[]{:S(2)}) collective-permute-start(f32[96,1024]{1,0:T(8,128)} %slice.148), channel_id=1, source_target_pairs={{1,0},{2,1},{3,2},{4,3},{5,4},{6,5},{7,6},{8,7},{9,8},{10,9},{11,1... | collective-permute-start | bytes 1179656 | tf_op jit(solution)/shard_map/ppermute | solution.py:17
  156.9 7.9 %copy-start.35 = (f32[3,8,48]{2,1,0:T(8,128)S(1)}, f32[3,8,48]{2,1,0:T(8,128)}, u32[]{:S(2)}) copy-start(f32[3,8,48]{2,1,0:T(8,128)} %copy-done.34) | copy-start | bytes 13828
  159.5 16.3 %collective-permute-start.3 = (f32[48,1024]{1,0:T(8,128)}, f32[48,1024]{1,0:T(8,128)}, u32[]{:S(2)}, u32[]{:S(2)}) collective-permute-start(f32[48,1024]{1,0:T(8,128)} %slice.150), channel_id=1, source_target_pairs={{0,1},{1,2},{2,3},{3,4},{4,5},{5,6},{6,7},{7,8},{8,9},{9,10},{10,1... | collective-permute-start | bytes 589832 | tf_op jit(solution)/shard_map/ppermute | solution.py:17
  164.7 10.6 %slice-start = ((f32[6,48,16,64]{3,2,1,0:T(8,128)}), f32[3,48,16,64]{3,2,1,0:T(8,128)S(1)}, s32[]{:S(2)}) async-start(f32[6,48,16,64]{3,2,1,0:T(8,128)} %copy-done.5), calls=%async_computation.4 | async-start | bytes 2359296 | tf_op jit(solution)/shard_map/slice | solution.py:147
  175.3 2.3 copy-start.7
  175.7 1.9 copy-start.27
  175.7 1.9 copy-start.30
  175.7 1.9 copy-start.32
  176.9 0.7 copy-start.24
  180.4 1.0 copy-start.12
  180.4 1.1 copy-start.14
  180.4 1.2 copy-start.16
  180.4 1.3 copy-start.18
  180.4 1.3 copy-start.36
  181.8 3.2 %copy-start.28 = (f32[1,1024]{1,0:T(1,128)S(1)}, f32[1,1024]{1,0:T(1,128)}, u32[]{:S(2)}) copy-start(f32[1,1024]{1,0:T(1,128)} %copy-done.26) | copy-start | bytes 12292
  181.8 3.2 %copy-start.33 = (f32[144]{0:T(256)S(1)}, f32[144]{0:T(256)}, u32[]{:S(2)}) copy-start(f32[144]{0:T(256)} %copy-done.31) | copy-start | bytes 1732
  248.5 10.0 %copy-start.10 = (bf16[64,1536]{1,0:T(8,128)(2,1)S(1)}, bf16[64,1536]{1,0:T(8,128)(2,1)}, u32[]{:S(2)}) copy-start(bf16[64,1536]{1,0:T(8,128)(2,1)} %reduce-scatter.2.cloned.1.call-done) | copy-start | bytes 589828
  249.6 9.0 %collective-permute-start.4 = (f32[64,1536]{1,0:T(8,128)S(1)}, f32[64,1536]{1,0:T(8,128)S(1)}, u32[]{:S(2)}, u32[]{:S(2)}) collective-permute-start(f32[64,1536]{1,0:T(8,128)S(1)} %convert_element_type.71), channel_id=1, source_target_pairs={{0,16},{16,0},{1,17},{17,1},{2,18},{18,2},{3,19},{19,3},{4,20},{20... | collective-permute-start | bytes 1179656 | tf_op jit(solution)/shard_map/ppermute | solution.py:168
Sparse Core Ops, SparseCore 0:
  10.3 42.7 all-gather.2
  55.9 44.2 all-gather.4
  180.6 67.9 reduce-scatter.1
